TPU v7x, 32 devices: a whole 2x2x4 slice. The times are simulated.
32 devices in a mesh: tile: 8 (over z, x), tp: 4 (over y, core).
Axes of the slice: x: 2, y: 2, z: 4, core: 2. Of those that a mesh axis runs over, the one named last changes fastest.
Arguments:
- latent: bfloat16 [512, 1024], P(('tile', 'tp')), may hold values from -6 to 6
- weight_in: bfloat16 [1024, 4096], P(None, 'tp'), may hold values from -0.1875 to 0.1875
- weight_out: bfloat16 [4096, 1024], P('tp'), may hold values from -0.09375 to 0.09375
- weight_conv: bfloat16 [7168, 2048], P(None, 'tp'), may hold values from -0.0625 to 0.0625
- neighbours: int32 [512, 7], P('tile'), may hold values from 0 to 96, as said below
- child_order: int32 [2048], P(('tile', 'tp')), may hold values from 0 to 63, as said below
- cotangent: bfloat16 [2048, 512], P(('tile', 'tp')), may hold values from -6 to 6
Outputs:
- fine_cells: bfloat16 [2048, 512], P(('tile', 'tp'))
- grad_latent: float32 [512, 1024], P(('tile', 'tp'))
- weight_in_grad: float32 [1024, 4096], P('tile', 'tp')
- weight_out_grad: float32 [4096, 1024], P('tp', 'tile')
- weight_conv_grad: float32 [7168, 2048], P('tile', 'tp')
Inputs may be any that keep to these rules, and one draw needn't show every extreme that they name: `neighbours`: column 0 of the row of a tile's i-th cell is i + 16 (the cell itself); the other columns lie within 16 of it, except that index 96, the empty row, marks a missing sixth neighbour of a pentagon cell. `child_order`: each block of 64 consecutive entries is a permutation of 0 .. 63.
All inputs are finite; a program needn't handle non-finite values.
Results may differ from a plain program's by a relative error of at most 0.02.
Values may be sent and summed in bfloat16 or wider, within the bound.
No kernel may reach another device: no remote copies, remote signals or barrier semaphores. Data moves between devices by JAX's collectives and lax.ppermute only.
A program may use at most 128 MiB of HBM per device.

v0:
```python
import math

import jax
import jax.numpy as jnp
from jax import lax
from jax.sharding import PartitionSpec as P

SLOTS = 4
HALO = 16


EPSILON = 1e-05


def with_halo(value, sides, width):
    for axis, dim in sides:
        count, length = (lax.axis_size(axis), value.shape[dim])
        up = [(i, (i + 1) % count) for i in range(count - 1)]
        down = [(j, i) for i, j in up]
        last = lax.slice_in_dim(value, length - width, length, axis=dim)
        initial = lax.slice_in_dim(value, 0, width, axis=dim)
        before = lax.ppermute(last, axis, up)
        after = lax.ppermute(initial, axis, down)
        value = jnp.concatenate([before, value, after], axis=dim)
    return value


def silu_grad(pre_value):
    sigmoid = jax.nn.sigmoid(pre_value)
    return sigmoid * (1.0 + pre_value * (1.0 - sigmoid))


def tp_rows(pieces):
    return lax.all_gather(pieces, "tp", axis=0, tiled=True)


def tp_sums(terms):
    return lax.psum(terms.astype(jnp.bfloat16), "tp").astype(jnp.float32)


def tile_margin(tile_data):
    return with_halo(tile_data, (("tile", 0),), HALO)


def regroup(block_data):
    return lax.all_to_all(block_data, "tp", split_axis=0, concat_axis=0, tiled=True)


def local(latent, weight_in, weight_out, weight_conv, neighbours, child_order, cotangent):
    groups = lax.axis_size("tp")
    tiles = lax.axis_size("tile")
    sub_rows = latent.shape[0]
    features = latent.shape[1]
    tile_rows = sub_rows * groups
    grad_scale = 1.0 / math.sqrt(tile_rows * tiles)
    tap_count = neighbours.shape[1]
    shard_cols = weight_conv.shape[1]
    shard_chans = shard_cols // SLOTS
    own_start = lax.axis_index("tp") * sub_rows
    source = latent.astype(jnp.float32)
    whole_source = tp_rows(latent).astype(jnp.float32)
    tile_norm = lax.rsqrt(jnp.mean(whole_source * whole_source, axis=1, keepdims=True) + EPSILON)
    norm_factor = lax.dynamic_slice_in_dim(tile_norm, own_start, sub_rows, 0)
    normed = (whole_source * tile_norm).astype(jnp.bfloat16)
    pre_act = jnp.dot(normed, weight_in, preferred_element_type=jnp.float32)
    hidden = jax.nn.silu(pre_act).astype(jnp.bfloat16)
    mixed = tp_sums(jnp.dot(hidden, weight_out, preferred_element_type=jnp.float32))
    latent_tile = (whole_source + mixed).astype(jnp.bfloat16)
    extended = jnp.concatenate(
        [tile_margin(latent_tile), jnp.zeros((1, features), jnp.bfloat16)], axis=0
    )
    tap_rows = jnp.take(extended, neighbours, axis=0).reshape(tile_rows, tap_count * features)
    coarse_out = jnp.dot(tap_rows, weight_conv, preferred_element_type=jnp.float32).astype(
        jnp.bfloat16
    )
    own_blocks = regroup(coarse_out)
    children = own_blocks.reshape(groups, sub_rows, shard_chans, SLOTS).transpose(1, 3, 0, 2)
    children = children.reshape(sub_rows * SLOTS, groups * shard_chans)
    activated = jax.nn.silu(children.astype(jnp.float32)).astype(jnp.bfloat16)
    fine_cells = jnp.take(activated, child_order, axis=0)
    child_grad = jnp.zeros_like(cotangent).at[child_order].set(cotangent)
    child_pre_grad = (
        child_grad.astype(jnp.float32) * silu_grad(children.astype(jnp.float32))
    ).astype(jnp.bfloat16)
    outgoing = child_pre_grad.reshape(sub_rows, SLOTS, groups, shard_chans).transpose(2, 0, 3, 1)
    coarse_grad = regroup(outgoing.reshape(groups * sub_rows, shard_cols))
    weight_conv_grad = lax.psum_scatter(
        (
            jnp.einsum("rk,rc->kc", tap_rows, coarse_grad, preferred_element_type=jnp.float32)
            * grad_scale
        ).astype(jnp.bfloat16),
        "tile",
        scatter_dimension=0,
        tiled=True,
    ).astype(jnp.float32)
    tap_grad = jnp.dot(coarse_grad, weight_conv.T, preferred_element_type=jnp.float32)
    tap_grad = tap_grad.reshape(tile_rows * tap_count, features)
    ext_grad = (
        jnp.zeros((tile_rows + 2 * HALO + 1, features), jnp.float32)
        .at[neighbours.reshape(-1)]
        .add(tap_grad)
    )
    rim_rows = jnp.concatenate(
        [ext_grad[:HALO], ext_grad[tile_rows + HALO : tile_rows + 2 * HALO]], axis=0
    ).astype(jnp.bfloat16)
    arrived = tile_margin(rim_rows).astype(jnp.float32)
    partial_value = ext_grad[HALO : HALO + tile_rows]
    partial_value = partial_value.at[:HALO].add(arrived[:HALO])
    partial_value = partial_value.at[tile_rows - HALO :].add(arrived[3 * HALO :])
    latent_grad = lax.psum_scatter(
        partial_value.astype(jnp.bfloat16), "tp", scatter_dimension=0, tiled=True
    ).astype(jnp.float32)
    upstream = tp_rows(latent_grad.astype(jnp.bfloat16))
    hidden_grad = jnp.dot(upstream, weight_out.T, preferred_element_type=jnp.float32)
    pre_grad = (hidden_grad * silu_grad(pre_act)).astype(jnp.bfloat16)
    out_term = (
        jnp.einsum("rf,rd->fd", hidden, upstream, preferred_element_type=jnp.float32) * grad_scale
    )
    weight_out_grad = lax.psum_scatter(
        out_term.astype(jnp.bfloat16), "tile", scatter_dimension=1, tiled=True
    ).astype(jnp.float32)
    normed_whole = tp_sums(jnp.dot(pre_grad, weight_in.T, preferred_element_type=jnp.float32))
    normed_grad = lax.dynamic_slice_in_dim(normed_whole, own_start, sub_rows, 0)
    grad_latent = (
        latent_grad
        + norm_factor * normed_grad
        - source
        * norm_factor
        * norm_factor
        * norm_factor
        * jnp.mean(normed_grad * source, axis=1, keepdims=True)
    )
    weight_in_grad = lax.psum_scatter(
        (
            jnp.einsum("rd,rf->df", normed, pre_grad, preferred_element_type=jnp.float32)
            * grad_scale
        ).astype(jnp.bfloat16),
        "tile",
        scatter_dimension=0,
        tiled=True,
    ).astype(jnp.float32)
    return (fine_cells, grad_latent, weight_in_grad, weight_out_grad, weight_conv_grad)


def solution(mesh):
    placed = (
        P(("tile", "tp"), None),
        P(None, "tp"),
        P("tp", None),
        P(None, "tp"),
        P("tile", None),
        P(("tile", "tp")),
        P(("tile", "tp"), None),
    )
    return jax.shard_map(
        local,
        mesh=mesh,
        in_specs=placed,
        out_specs=(
            P(("tile", "tp"), None),
            P(("tile", "tp"), None),
            P("tile", "tp"),
            P("tp", "tile"),
            P("tile", "tp"),
        ),
        check_vma=False,
    )
```

profile of v0, /device:TPU:0, one launch (start us, length us, event | category | flops | bytes accessed | tf_op | source)
XLA Modules:
  0.0 469.5 jit_solution(18033173362639526849)
XLA Ops:
  7.2 6.9 %all_gather.6 = bf16[64,1024]{1,0:T(8,128)(2,1)S(1)} all-gather(bf16[16,1024]{1,0:T(8,128)(2,1)} %param.11), channel_id=1, replica_groups=mesh['tile'=8,'tp'=4] {'tp'}, dimensions={0}, use_global_device_ids=true | all-gather | bytes 163840 | tf_op jit(solution)/shard_map/all_gather | solution.py:34
  14.3 2.1 fusion.23
  16.4 1.1 convolution_convert_fusion.1
  17.8 33.3 %all-reduce.3.cloned.1.call-done = bf16[64,1024]{1,0:T(8,128)(2,1)} async-done(((bf16[64,1024]{1,0:T(8,128)(2,1)}), bf16[64,1024]{1,0:T(8,128)(2,1)}) %all-reduce.3.cloned.1.call-update) | async-done | bytes 131088 | tf_op jit(solution)/shard_map/psum | solution.py:38
  51.1 0.9 fusion.3
  52.1 3.4 collective-permute-start
  55.4 1.3 collective-permute-start.1
  57.0 4.2 collective-permute-done.1
  61.4 2.7 gather_fusion
  64.1 2.2 reshape.167
  66.3 1.4 broadcast_select_fusion
  68.3 5.1 %convolution_convert_fusion.2 = bf16[64,512]{1,0:T(8,128)(2,1)} fusion(bf16[64,7168]{1,0:T(8,128)(2,1)S(1)} %bitcast.55, bf16[7168,512]{1,0:T(8,128)(2,1)} %param.14), kind=kOutput, calls=%fused_computation.11 | convolution fusion | flops 469794816 | bytes 8323072 | tf_op jit(solution)/shard_map/dot_general | solution.py:73
  73.4 3.3 all-to-all-start
  77.0 1.2 scatter_custom_fusion
  78.1 2.7 all-to-all-done
  80.8 1.2 copy.29
  82.0 1.5 copy.30
  83.6 1.1 copy.32
  84.7 1.8 copy.33
  86.6 3.3 all-to-all-start.1
  89.9 4.0 all-to-all-done.1
  93.9 6.6 %fusion.29 = f32[64,7168]{1,0:T(8,128)} fusion(bf16[64,512]{1,0:T(8,128)(2,1)S(1)} %bitcast.61, bf16[7168,512]{1,0:T(8,128)(2,1)} %param.14), kind=kOutput, calls=%fused_computation.66 | convolution fusion | flops 469762048 | bytes 9240576 | tf_op jit(solution)/shard_map/dot_general | solution.py:96
  100.6 2.7 reshape.194
  103.3 5.8 %scatter_custom_fusion.1 = f32[97,1024]{1,0:T(8,128)} fusion(s32[448]{0:T(512)S(1)} %bitcast.65, f32[448,1024]{1,0:T(8,128)} %reshape.194, f32[]{:T(128)} %constant.110.clone.1), kind=kCustom, calls=%fused_computation.22 | custom fusion | flops 458752 | bytes 397824 | tf_op jit(solution)/shard_map/scatter-add | solution.py:101
  109.1 1.0 convert.9
  110.1 4.3 collective-permute-start.2
  114.4 1.3 collective-permute-start.3
  115.7 1.0 slice.79
  116.7 3.5 collective-permute-done.3
  120.2 0.8 fusion.21
  121.8 18.8 %reduce-scatter.7.cloned.1.call-done = bf16[16,1024]{1,0:T(8,128)(2,1)} async-done(((bf16[64,1024]{1,0:T(8,128)(2,1)}), bf16[16,1024]{1,0:T(8,128)(2,1)}) %reduce-scatter.7.cloned.1.call-update) | async-done | bytes 32784 | tf_op jit(solution)/shard_map/reduce_scatter | solution.py:110
  140.7 5.9 %all_gather.7 = bf16[64,1024]{1,0:T(8,128)(2,1)S(1)} all-gather(bf16[16,1024]{1,0:T(8,128)(2,1)} %reduce-scatter.7.cloned.1.call-done), channel_id=1, replica_groups=mesh['tile'=8,'tp'=4] {'tp'}, dimensions={0}, use_global_device_ids=true | all-gather | bytes 163840 | tf_op jit(solution)/shard_map/all_gather | solution.py:34
  146.6 1.7 fusion
  148.3 1.4 convolution_convert_fusion
  149.8 3.1 multiply_convert_fusion.1
  152.9 4.0 copy.34
  156.9 2.1 multiply_convert_fusion.2
  159.1 5.1 %multiply_convert_fusion = bf16[7168,512]{1,0:T(8,128)(2,1)} fusion(bf16[64,7168]{1,0:T(8,128)(2,1)S(1)} %bitcast.56, bf16[64,512]{1,0:T(8,128)(2,1)S(1)} %bitcast.62), kind=kOutput, calls=%fused_computation.4 | convolution fusion | flops 477102080 | bytes 8323072 | tf_op jit(solution)/shard_map/rk,rc->kc/dot_general | solution.py:89
  165.7 16.0 %all-reduce.5.cloned.1.call-done = bf16[64,1024]{1,0:T(8,128)(2,1)} async-done(((bf16[64,1024]{1,0:T(8,128)(2,1)}), bf16[64,1024]{1,0:T(8,128)(2,1)}) %all-reduce.5.cloned.1.call-update) | async-done | bytes 131088 | tf_op jit(solution)/shard_map/psum | solution.py:38
  181.7 0.9 fusion.19
  182.6 1.5 fusion.15
  184.1 69.7 %reduce-scatter.13.cloned.1.call-done = bf16[128,1024]{1,0:T(8,128)(2,1)} async-done(((bf16[1024,1024]{1,0:T(8,128)(2,1)}), bf16[128,1024]{1,0:T(8,128)(2,1)}) %reduce-scatter.13.cloned.1.call-update) | async-done | bytes 262160
  253.8 1.1 copy.35
  254.9 0.8 convert_element_type.108
  255.8 68.8 %reduce-scatter.9.cloned.1.call-done = bf16[128,1024]{1,0:T(8,128)(2,1)} async-done(((bf16[1024,1024]{1,0:T(8,128)(2,1)}), bf16[128,1024]{1,0:T(8,128)(2,1)}) %reduce-scatter.9.cloned.1.call-update) | async-done | bytes 262160 | tf_op jit(solution)/shard_map/reduce_scatter | solution.py:133
  324.6 1.8 convert_element_type.106
  326.4 133.6 %reduce-scatter.11.cloned.1.call-done = bf16[896,512]{1,0:T(8,128)(2,1)} async-done(((bf16[7168,512]{1,0:T(8,128)(2,1)}), bf16[896,512]{1,0:T(8,128)(2,1)}) %reduce-scatter.11.cloned.1.call-update) | async-done | bytes 917520 | tf_op jit(solution)/shard_map/reduce_scatter | solution.py:87
  460.0 2.7 convert_element_type.110
  (55 shorter events, 4.3 us)
Async XLA Ops:
  7.2 9.2 %copy-start = (bf16[1024,1024]{1,0:T(8,128)(2,1)S(1)}, bf16[1024,1024]{1,0:T(8,128)(2,1)}, u32[]{:S(2)}) copy-start(bf16[1024,1024]{1,0:T(8,128)(2,1)} %param.13) | copy-start | bytes 6291460
  7.2 43.9 %all-reduce.3.cloned.1.call-start = ((), (), s32[]{:S(2)}) async-start(), calls=%async_computation.6 | async-start | bytes 262144 | tf_op jit(solution)/shard_map/psum | solution.py:38
  14.2 3.3 copy-start.5
  16.4 1.4 copy-start.3
  52.1 5.0 %collective-permute-start = (bf16[16,1024]{1,0:T(8,128)(2,1)S(1)}, bf16[16,1024]{1,0:T(8,128)(2,1)S(1)}, u32[]{:S(2)}, u32[]{:S(2)}) collective-permute-start(bf16[16,1024]{1,0:T(8,128)(2,1)S(1)} %get-tuple-element.33), channel_id=1, source_target_pairs={{0,4},{4,8},{8,12},{12,16},{16,20},{20,24},{24,28},{1,5},{5,9},{9,... | collective-permute-start | bytes 98312 | tf_op jit(solution)/shard_map/ppermute | solution.py:22
  55.4 5.8 %collective-permute-start.1 = (bf16[16,1024]{1,0:T(8,128)(2,1)S(1)}, bf16[16,1024]{1,0:T(8,128)(2,1)S(1)}, u32[]{:S(2)}, u32[]{:S(2)}) collective-permute-start(bf16[16,1024]{1,0:T(8,128)(2,1)S(1)} %get-tuple-element.34), channel_id=1, source_target_pairs={{4,0},{8,4},{12,8},{16,12},{20,16},{24,20},{28,24},{5,1},{9,5},{13... | collective-permute-start | bytes 98312 | tf_op jit(solution)/shard_map/ppermute | solution.py:23
  68.3 8.4 %copy-start.6 = (s32[64]{0:T(128)S(1)}, s32[64]{0:T(128)}, u32[]{:S(2)}) copy-start(s32[64]{0:T(128)} %param.16) | copy-start | bytes 772
  73.4 7.4 %all-to-all-start = ((bf16[4,16,512]{2,1,0:T(8,128)(2,1)}), bf16[4,16,512]{2,1,0:T(8,128)(2,1)S(1)}, u32[]{:S(2)}, u32[]{:S(2)}) async-start(bf16[4,16,512]{2,1,0:T(8,128)(2,1)} %bitcast), calls=%async_computation | async-start | bytes 131072 | tf_op jit(solution)/shard_map/all_to_all | solution.py:46
  86.6 7.4 %all-to-all-start.1 = ((bf16[4,16,512]{2,1,0:T(8,128)(2,1)}), bf16[4,16,512]{2,1,0:T(8,128)(2,1)S(1)}, u32[]{:S(2)}, u32[]{:S(2)}) async-start(bf16[4,16,512]{2,1,0:T(8,128)(2,1)} %copy.33), calls=%async_computation.1 | async-start | bytes 131072 | tf_op jit(solution)/shard_map/all_to_all | solution.py:46
  89.9 50.8 %reduce-scatter.7.cloned.1.call-start = ((), (), s32[]{:S(2)}) async-start(), calls=%async_computation.7 | async-start | bytes 163840 | tf_op jit(solution)/shard_map/reduce_scatter | solution.py:110
  110.1 6.6 %collective-permute-start.2 = (bf16[16,1024]{1,0:T(8,128)(2,1)S(1)}, bf16[16,1024]{1,0:T(8,128)(2,1)S(1)}, u32[]{:S(2)}, u32[]{:S(2)}) collective-permute-start(bf16[16,1024]{1,0:T(8,128)(2,1)S(1)} %get-tuple-element.29), channel_id=1, source_target_pairs={{0,4},{4,8},{8,12},{12,16},{16,20},{20,24},{24,28},{1,5},{5,9},{9,... | collective-permute-start | bytes 98312 | tf_op jit(solution)/shard_map/ppermute | solution.py:22
  114.4 5.8 %collective-permute-start.3 = (bf16[16,1024]{1,0:T(8,128)(2,1)S(1)}, bf16[16,1024]{1,0:T(8,128)(2,1)S(1)}, u32[]{:S(2)}, u32[]{:S(2)}) collective-permute-start(bf16[16,1024]{1,0:T(8,128)(2,1)S(1)} %get-tuple-element.30), channel_id=1, source_target_pairs={{4,0},{8,4},{12,8},{16,12},{20,16},{24,20},{28,24},{5,1},{9,5},{13... | collective-permute-start | bytes 98312 | tf_op jit(solution)/shard_map/ppermute | solution.py:23
  121.8 59.9 %all-reduce.5.cloned.1.call-start = ((), (), s32[]{:S(2)}) async-start(), calls=%async_computation.8 | async-start | bytes 262144 | tf_op jit(solution)/shard_map/psum | solution.py:38
  140.7 7.6 %copy-start.1 = (bf16[1024,1024]{1,0:T(8,128)(2,1)S(1)}, bf16[1024,1024]{1,0:T(8,128)(2,1)}, u32[]{:S(2)}) copy-start(bf16[1024,1024]{1,0:T(8,128)(2,1)} %param.12) | copy-start | bytes 6291460
  149.8 104.0 %reduce-scatter.13.cloned.1.call-start = ((), (), s32[]{:S(2)}) async-start(), calls=%async_computation.11 | async-start | bytes 2359296
  156.9 167.7 %reduce-scatter.9.cloned.1.call-start = ((), (), s32[]{:S(2)}) async-start(), calls=%async_computation.9 | async-start | bytes 2359296 | tf_op jit(solution)/shard_map/reduce_scatter | solution.py:133
  159.1 300.9 %reduce-scatter.11.cloned.1.call-start = ((), (), s32[]{:S(2)}) async-start(), calls=%async_computation.10 | async-start | bytes 8257536 | tf_op jit(solution)/shard_map/reduce_scatter | solution.py:87
  164.2 17.5 %copy-start.2 = (bf16[16,1024]{1,0:T(8,128)(2,1)S(1)}, bf16[16,1024]{1,0:T(8,128)(2,1)}, u32[]{:S(2)}) copy-start(bf16[16,1024]{1,0:T(8,128)(2,1)} %param.11) | copy-start | bytes 98308
  164.2 18.4 %copy-start.4 = (bf16[16,1024]{1,0:T(8,128)(2,1)S(1)}, bf16[16,1024]{1,0:T(8,128)(2,1)}, u32[]{:S(2)}) copy-start(bf16[16,1024]{1,0:T(8,128)(2,1)} %reduce-scatter.7.cloned.1.call-done) | copy-start | bytes 98308
Sparse Core Ops, SparseCore 0:
  17.7 33.3 all-reduce.2
  121.9 18.7 reduce-scatter.6
  149.9 31.7 all-reduce.4
  185.1 68.6 reduce-scatter.12
  257.2 67.3 reduce-scatter.8
  328.0 131.9 reduce-scatter.10
where the time goes:
time: 471 us; the launch traced here: 470 us
  waiting for transfers between devices  355 us (75%)
  matrix products  28.4 us (6%)
  local copies, waits for them, and re-layouts  22.6 us (5%)
  other arithmetic  19.4 us (4%)
  starting transfers between devices  17.1 us (4%)
  between operations  14.4 us (3%)
  blocking collectives  12.8 us (3%)
    reduce_scatter x1, waiting for transfers between devices, local(): lax.psum_scatter((jnp.einsum('rk,rc->kc', tap_rows, coarse_grad, preferre...  134 us
    unnamed x7, waiting for transfers between devices  69.8 us
    reduce_scatter x1, waiting for transfers between devices, local(): lax.psum_scatter((jnp.einsum('rd,rf->df', normed, pre_grad, preferred_ele...  68.8 us
    psum x2, waiting for transfers between devices, tp_sums(): return lax.psum(terms.astype(jnp.bfloat16), 'tp').astype(jnp.float32)  49.2 us
    reduce_scatter x1, waiting for transfers between devices, local(): lax.psum_scatter(partial_value.astype(jnp.bfloat16), 'tp', scatter_dimens...  18.8 us
    all_gather x2, blocking collectives, tp_rows(): return lax.all_gather(pieces, 'tp', axis=0, tiled=True)  12.8 us
  transfers between devices with their start and end apart: 12, of which 11 were waited for; matrix products, arithmetic and copies ran while one was open for 5% of the time, Pallas kernels for 0%

commit v1 on v0

v1 whole, which is shorter than its diff:
```python
import functools
import math

import jax
import jax.numpy as jnp
from jax import lax
from jax.experimental import pallas as pl
from jax.experimental.pallas import tpu as pltpu
from jax.sharding import PartitionSpec as P

SLOTS = 4
HALO = 16
EPSILON = 1e-05
ABSENT = 100.0
BF = jnp.bfloat16
F32 = jnp.float32


def silu_grad(pre_value):
    sigmoid = jax.nn.sigmoid(pre_value)
    return sigmoid * (1.0 + pre_value * (1.0 - sigmoid))


def dot(a, b, dims=((1,), (0,))):
    return lax.dot_general(a, b, (dims, ((), ())), preferred_element_type=F32)


def flip(value, bit):
    count = lax.axis_size("tp")
    return lax.ppermute(value, "tp", [(i, i ^ bit) for i in range(count)])


def higher_bits():
    bits, bit = [], 2
    while bit < lax.axis_size("tp"):
        bits.append(bit)
        bit *= 2
    return bits


def to_all_tiles(value):
    tiles = lax.axis_size("tile")
    copies = jnp.broadcast_to(value[None], (tiles, *value.shape))
    return lax.all_to_all(copies, "tile", split_axis=0, concat_axis=0, tiled=True)


def tap_of(table, k):
    lanes = lax.broadcasted_iota(jnp.int32, table.shape, 1)
    return jnp.sum(jnp.where(lanes == k, table, 0.0), axis=1, keepdims=True)


def conv_forward(rows_ref, table_ref, cot_ref, weight_ref, grad_ref, act_ref, acc_ref, *, halo):
    k = pl.program_id(0)

    @pl.when(k == 0)
    def _():
        acc_ref[...] = jnp.zeros_like(acc_ref)

    target = tap_of(table_ref[...], k).astype(jnp.int32)
    cells, window = acc_ref.shape[0], rows_ref.shape[0]
    pick = lax.broadcasted_iota(jnp.int32, (cells, window), 1) == target
    taps = dot(pick.astype(F32).astype(BF), rows_ref[...]).astype(BF)
    acc_ref[...] += dot(taps, weight_ref[...])

    @pl.when(k == pl.num_programs(0) - 1)
    def _():
        value = acc_ref[...].astype(BF).astype(F32)
        sigmoid = jax.nn.sigmoid(value)
        slope = sigmoid * (1.0 + value * (1.0 - sigmoid))
        grad_ref[...] = (cot_ref[...].astype(F32) * slope).astype(BF)
        act = (value * sigmoid).astype(BF)
        act_ref[...] = act[halo : cells - halo]


def conv_backward(grad_ref, table_ref, order_ref, weight_ref, out_ref, acc_ref):
    k = pl.program_id(0)

    @pl.when(k == 0)
    def _():
        acc_ref[...] = jnp.zeros_like(acc_ref)

    target = tap_of(table_ref[...], k).astype(jnp.int32)
    pick = (order_ref[0:1, :] == target).astype(F32).astype(BF)
    summed = dot(pick, grad_ref[...], ((0,), (0,))).astype(BF)
    acc_ref[...] += dot(summed, weight_ref[...], ((1,), (1,)))

    @pl.when(k == pl.num_programs(0) - 1)
    def _():
        out_ref[...] = acc_ref[...].astype(BF)


def whole(shape):
    return pl.BlockSpec(shape, lambda k: (0,) * len(shape))


def run_conv_forward(rows, table, cot, weight, features):
    cells, cols = cot.shape
    taps = weight.shape[0] // features
    return pl.pallas_call(
        functools.partial(conv_forward, halo=HALO),
        grid=(taps,),
        in_specs=[
            whole(rows.shape),
            whole(table.shape),
            whole(cot.shape),
            pl.BlockSpec((features, cols), lambda k: (k, 0)),
        ],
        out_specs=[whole((cells, cols)), whole((cells - 2 * HALO, cols))],
        out_shape=[
            jax.ShapeDtypeStruct((cells, cols), BF),
            jax.ShapeDtypeStruct((cells - 2 * HALO, cols), BF),
        ],
        scratch_shapes=[pltpu.VMEM((cells, cols), F32)],
        name="conv_forward",
    )(rows, table, cot, weight)


def run_conv_backward(grad, table, order, weight, features):
    cells, cols = grad.shape
    taps = weight.shape[0] // features
    out = (order.shape[1], features)
    return pl.pallas_call(
        conv_backward,
        grid=(taps,),
        in_specs=[
            whole(grad.shape),
            whole(table.shape),
            whole(order.shape),
            pl.BlockSpec((features, cols), lambda k: (k, 0)),
        ],
        out_specs=whole(out),
        out_shape=jax.ShapeDtypeStruct(out, BF),
        scratch_shapes=[pltpu.VMEM(out, F32)],
        name="conv_backward",
    )(grad, table, order, weight)


def local(latent, weight_in, weight_out, weight_conv, neighbours, child_order, cotangent):
    groups = lax.axis_size("tp")
    tiles = lax.axis_size("tile")
    sub, features = latent.shape
    tile_rows = sub * groups
    tap_count = neighbours.shape[1]
    cols = weight_conv.shape[1]
    chans = cols // SLOTS
    grad_scale = 1.0 / math.sqrt(tile_rows * tiles)
    member = lax.axis_index("tp")
    tile = lax.axis_index("tile")
    core = member % 2
    half = tile_rows // 2
    assert sub == HALO and groups >= 4

    row_ids = jnp.arange(tile_rows, dtype=jnp.int32)[:, None]
    offsets = jnp.where(
        neighbours == tile_rows + 2 * HALO, ABSENT, (neighbours - row_ids - HALO).astype(F32)
    )
    offsets = jnp.pad(offsets, ((0, 0), (0, 128 - tap_count))).astype(BF)
    own_offsets = lax.dynamic_slice_in_dim(offsets, member * sub, sub, 0)
    packed = jnp.concatenate([latent, own_offsets], axis=1)

    last = groups - 1
    hops = [((t + 1) * groups + p, t * groups + p) for t in range(tiles - 1) for p in (0, 1)]
    hops += [(t * groups + p, (t + 1) * groups + p) for t in range(tiles - 1) for p in (last - 1, last)]
    beside = lax.ppermute(packed, ("tile", "tp"), hops)
    blocks = lax.all_gather(jnp.concatenate([packed, beside], axis=0), "tp", axis=0, tiled=False)
    own_rows = blocks[:, :sub].reshape(tile_rows, -1)
    left = blocks[groups - 2 :, sub:].reshape(2 * sub, -1)
    right = blocks[:2, sub:].reshape(2 * sub, -1)
    window = jnp.concatenate([left, own_rows, right], axis=0)
    source = window[:, :features].astype(F32)
    cells = tile_rows + 2 * HALO
    cell_ids = jnp.arange(cells, dtype=F32)[:, None]
    table = window[HALO : HALO + cells, features:].astype(F32)
    table = jnp.where(table == ABSENT, -1.0, table + cell_ids + HALO)

    fine_rows = sub * SLOTS
    fine_ids = jnp.arange(fine_rows, dtype=jnp.int32)
    fine_of = SLOTS * (fine_ids % sub) + fine_ids // sub
    chosen = (child_order[None, :] == fine_of[:, None]).astype(BF)
    child_grad = dot(chosen, cotangent).astype(BF)
    child_hops = [h for h in hops if h[0] % groups in (0, last)]
    child_beside = lax.ppermute(child_grad, ("tile", "tp"), child_hops)
    both = jnp.stack([child_grad, child_beside])
    both = both.reshape(2 * fine_rows, groups, chans).transpose(1, 0, 2)
    arrived = lax.all_to_all(both, "tp", split_axis=0, concat_axis=0, tiled=True)
    arrived = arrived.reshape(groups, 2, SLOTS, sub, chans)
    in_order = jnp.concatenate(
        [arrived[last:, 1], arrived[:, 0], arrived[:1, 1]], axis=0
    )
    in_order = in_order.transpose(0, 2, 1, 3).reshape(cells, cols)
    col_ids = jnp.arange(cols, dtype=jnp.int32)
    col_from = (col_ids % SLOTS) * chans + col_ids // SLOTS
    reorder = (col_ids[:, None] == col_from[None, :]).astype(BF)
    cot = dot(in_order, reorder).astype(BF)

    factor = lax.rsqrt(jnp.mean(source * source, axis=1, keepdims=True) + EPSILON)
    normed = (source * factor).astype(BF)
    pre_act = dot(normed, weight_in)
    hidden = jax.nn.silu(pre_act).astype(BF)
    mixed = dot(hidden, weight_out).astype(BF)
    for bit in [1] + higher_bits():
        mixed_sum = mixed.astype(F32) + flip(mixed, bit).astype(F32)
        mixed = mixed_sum.astype(BF)
    latent_out = (source + mixed_sum).astype(BF)

    coarse_grad, activated = run_conv_forward(latent_out, table, cot, weight_conv, features)

    row_of = jnp.arange(half, dtype=jnp.int32)
    kept = (row_of // sub) * 2 * sub + row_of % sub + core * sub
    given = (row_of // sub) * 2 * sub + row_of % sub + (1 - core) * sub
    order = jnp.concatenate([kept, given])
    order_rows = jnp.broadcast_to((order + 2 * HALO)[None, :], (8, tile_rows))
    partial_value = run_conv_backward(coarse_grad, table, order_rows, weight_conv, features)

    value = partial_value[:half].astype(F32) + flip(partial_value[half:], 1).astype(F32)
    for bit in higher_bits():
        piece = value.astype(BF)
        value = piece.astype(F32) + flip(piece, bit).astype(F32)
    latent_grad = value
    upstream = latent_grad.astype(BF)
    other_upstream = flip(upstream, 1)

    def own_half(rows):
        parts = rows.reshape(groups // 2, 2, sub, rows.shape[1])
        return lax.dynamic_index_in_dim(parts, core, 1, keepdims=False).reshape(half, -1)

    def other_half(rows):
        parts = rows.reshape(groups // 2, 2, sub, rows.shape[1])
        return lax.dynamic_index_in_dim(parts, 1 - core, 1, keepdims=False).reshape(half, -1)

    packed_mine = to_all_tiles(own_half(own_rows))
    packed_other = flip(packed_mine, 1)
    out_rows = latent_out[2 * HALO : 2 * HALO + tile_rows]
    out_mine = to_all_tiles(own_half(out_rows))
    out_other = flip(out_mine, 1)
    coarse_grads = to_all_tiles(coarse_grad[HALO : HALO + tile_rows])
    up_mine = to_all_tiles(upstream)
    up_other = flip(up_mine, 1)

    own_pre = pre_act[2 * HALO : 2 * HALO + tile_rows]
    own_slope = silu_grad(jnp.concatenate([own_half(own_pre), other_half(own_pre)], axis=0))
    up_rows = jnp.concatenate([upstream, other_upstream], axis=0)
    own_pre_grad = (dot(up_rows, weight_out, ((1,), (1,))) * own_slope).astype(BF)
    normed_part = dot(own_pre_grad, weight_in, ((1,), (1,))).astype(BF)
    block = member // 2
    normed_sum = normed_part[:half].astype(F32) + flip(normed_part[half:], 1).astype(F32)
    rows_left, index = normed_sum, block
    for bit in reversed(higher_bits()):
        piece = rows_left.astype(BF)
        count = piece.shape[0] // 2
        upper = (member // bit) % 2
        keep = lax.dynamic_slice_in_dim(piece, upper * count, count, 0)
        give = lax.dynamic_slice_in_dim(piece, (1 - upper) * count, count, 0)
        rows_left = keep.astype(F32) + flip(give, bit).astype(F32)
    normed_grad = rows_left
    own_source = latent.astype(F32)
    own_factor = lax.rsqrt(jnp.mean(own_source * own_source, axis=1, keepdims=True) + EPSILON)
    own_latent_grad = lax.dynamic_slice_in_dim(latent_grad, block * sub, sub, 0)
    grad_latent = (
        own_latent_grad
        + own_factor * normed_grad
        - own_source
        * own_factor
        * own_factor
        * own_factor
        * jnp.mean(normed_grad * own_source, axis=1, keepdims=True)
    )

    by_slot = dot(activated, reorder, ((1,), (1,))).astype(BF)
    by_slot = lax.all_to_all(
        by_slot.reshape(groups, sub, cols), "tp", split_axis=0, concat_axis=0, tiled=True
    )
    children = by_slot.reshape(groups, sub, SLOTS, chans).transpose(2, 1, 0, 3)
    children = children.reshape(fine_rows, groups * chans)
    fine_cells = dot(chosen, children, ((0,), (0,))).astype(BF)

    def halves(mine, other):
        return jnp.concatenate([mine, other], axis=0).reshape(2 * tiles * half, -1)

    packed_all = halves(packed_mine, packed_other)
    source_all = packed_all[:, :features].astype(F32)
    factor_all = lax.rsqrt(jnp.mean(source_all * source_all, axis=1, keepdims=True) + EPSILON)
    normed_all = (source_all * factor_all).astype(BF)
    pre_all = dot(normed_all, weight_in)
    hidden_all = jax.nn.silu(pre_all).astype(BF)
    up_all = halves(up_mine, up_other)
    pre_grad_all = (dot(up_all, weight_out, ((1,), (1,))) * silu_grad(pre_all)).astype(BF)
    d_cols = features // tiles
    normed_cols = lax.dynamic_slice_in_dim(normed_all, tile * d_cols, d_cols, 1)
    weight_in_grad = dot(normed_cols, pre_grad_all, ((0,), (0,))) * grad_scale
    up_cols = lax.dynamic_slice_in_dim(up_all, tile * d_cols, d_cols, 1)
    weight_out_grad = dot(hidden_all, up_cols, ((0,), (0,))) * grad_scale

    def natural(mine, other):
        even = jnp.where(core == 0, mine, other).reshape(tiles, groups // 2, sub, -1)
        odd = jnp.where(core == 0, other, mine).reshape(tiles, groups // 2, sub, -1)
        return jnp.stack([even, odd], axis=2).reshape(tiles, tile_rows, -1)

    out_all = natural(out_mine, out_other)
    offsets_all = natural(packed_mine[..., features:], packed_other[..., features:]).astype(F32)
    rim = jnp.zeros_like(out_all[:1, :HALO])
    before = jnp.concatenate([rim, out_all[:-1, tile_rows - HALO :]], axis=0)
    after = jnp.concatenate([out_all[1:, :HALO], rim], axis=0)
    extended = jnp.concatenate([before, out_all, after], axis=1)
    share = tap_count * features // tiles
    first = (tile * share) // features
    start = tile * share - first * features
    ext_ids = jnp.arange(cells, dtype=F32)[None, None, :]

    def taps_at(k):
        offset = lax.dynamic_slice_in_dim(offsets_all, k, 1, 2)
        target = offset + jnp.arange(tile_rows, dtype=F32)[None, :, None] + HALO
        target = jnp.where(offset == ABSENT, -1.0, target)
        pick = (ext_ids == target).astype(BF)
        picked = lax.dot_general(
            pick, extended, (((2,), (1,)), ((0,), (0,))), preferred_element_type=F32
        )
        return picked.astype(BF).reshape(tiles * tile_rows, features)

    pair = jnp.concatenate([taps_at(first), taps_at(jnp.minimum(first + 1, tap_count - 1))], axis=1)
    own_taps = lax.dynamic_slice_in_dim(pair, start, share, 1)
    grads_all = coarse_grads.reshape(tiles * tile_rows, cols)
    weight_conv_grad = dot(own_taps, grads_all, ((0,), (0,))) * grad_scale
    return (fine_cells, grad_latent, weight_in_grad, weight_out_grad, weight_conv_grad)


def solution(mesh):
    placed = (
        P(("tile", "tp"), None),
        P(None, "tp"),
        P("tp", None),
        P(None, "tp"),
        P("tile", None),
        P(("tile", "tp")),
        P(("tile", "tp"), None),
    )
    return jax.shard_map(
        local,
        mesh=mesh,
        in_specs=placed,
        out_specs=(
            P(("tile", "tp"), None),
            P(("tile", "tp"), None),
            P("tile", "tp"),
            P("tp", "tile"),
            P("tile", "tp"),
        ),
        check_vma=False,
    )
```

time: 471 us -> 151 us (0.32)
  waiting for transfers between devices: 355 us -> 40.4 us
  Pallas kernels: 0 us -> 16 us
  between operations: 14.4 us -> 1.02 us
  starting transfers between devices: 17.1 us -> 29.7 us
  local copies, waits for them, and re-layouts: 22.6 us -> 11.3 us
  blocking collectives: 12.8 us -> 7.98 us
    reduce_scatter x3 -> x0, waiting for transfers between devices: 221 us -> none  [the longest x1 134 us: local(): lax.psum_scatter((jnp.einsum('rk,rc->kc', tap_rows, coarse_grad, preferre...]
    unnamed x7 -> x0, waiting for transfers between devices: 69.8 us -> none
    psum x2 -> x0, waiting for transfers between devices: 49.2 us -> none  [tp_sums(): return lax.psum(terms.astype(jnp.bfloat16), 'tp').astype(jnp.float32)]
    all_to_all x2 -> x6, waiting for transfers between devices: 6.69 us -> 29.2 us  [the longest x4 21.2 us: to_all_tiles(): lax.all_to_all(copies, 'tile', split_axis=0, concat_axis=0, tiled=True)]
    all_to_all x2 -> x6, starting transfers between devices: 6.57 us -> 24.5 us  [the longest x4 17.9 us: to_all_tiles(): lax.all_to_all(copies, 'tile', split_axis=0, concat_axis=0, tiled=True)]
    pallas_call x0 -> x2, Pallas kernels: none -> 16 us  [the longest x1 8.23 us: run_conv_backward(): pl.pallas_call(conv_backward, grid=(taps,), in_specs=[whole(grad.shape),...]
    scatter-add x3 -> x0, other arithmetic: 6.69 us -> none  [the longest x1 5.83 us: local(): ext_grad = jnp.zeros((tile_rows + 2 * HALO + 1, features), jnp.float32).a...]
    gather x3 -> x0, local copies, waits for them, and re-layouts: 5.66 us -> none  [the longest x2 4.96 us: local(): jnp.take(extended, neighbours, axis=0)]
  transfers between devices with their start and end apart: 12 -> 18, of which waited for: 11 -> 10; matrix products, arithmetic and copies ran while one was open for 5% -> 25% of each run, Pallas kernels for 0% -> 6%
where the time goes in v1:
time: 151 us; the launch traced here: 149 us
  waiting for transfers between devices  40.4 us (27%)
  starting transfers between devices  29.7 us (20%)
  matrix products  26.4 us (17%)
  other arithmetic  16.4 us (11%)
  Pallas kernels  16 us (11%)
  local copies, waits for them, and re-layouts  11.3 us (7%)
  blocking collectives  7.98 us (5%)
    dot_general x11, matrix products, dot(): return lax.dot_general(a, b, (dims, ((), ())), preferred_element_type=F32)  23.4 us
    all_to_all x4, waiting for transfers between devices, to_all_tiles(): lax.all_to_all(copies, 'tile', split_axis=0, concat_axis=0, tiled=True)  21.2 us
    all_to_all x4, starting transfers between devices, to_all_tiles(): lax.all_to_all(copies, 'tile', split_axis=0, concat_axis=0, tiled=True)  17.9 us
    pallas_call x1, Pallas kernels, run_conv_backward(): pl.pallas_call(conv_backward, grid=(taps,), in_specs=[whole(grad.shape),...  8.23 us
    ppermute x10, waiting for transfers between devices, flip(): return lax.ppermute(value, 'tp', [(i, i ^ bit) for i in range(count)])  8.07 us
    all_gather x1, blocking collectives, local(): lax.all_gather(jnp.concatenate([packed, beside], axis=0), 'tp', axis=0, t...  7.98 us
    pallas_call x1, Pallas kernels, run_conv_forward(): pl.pallas_call(functools.partial(conv_forward, halo=HALO), grid=(taps,),...  7.76 us
    all_to_all x1, waiting for transfers between devices, local(): lax.all_to_all(by_slot.reshape(groups, sub, cols), 'tp', split_axis=0, co...  4.06 us
  transfers between devices with their start and end apart: 18, of which 10 were waited for; matrix products, arithmetic and copies ran while one was open for 25% of the time, Pallas kernels for 6%

profile of v1, /device:TPU:0, one launch (start us, length us, event | category | flops | bytes accessed | tf_op | source)
XLA Modules:
  0.0 149.2 jit_solution(4930725531376631672)
XLA Ops:
  0.7 0.8 select_convert_fusion
  2.4 1.3 collective-permute-start
  3.7 1.1 convolution_convert_fusion.6
  4.8 1.3 collective-permute-start.3
  6.1 3.1 %collective-permute-done = bf16[16,1152]{1,0:T(8,128)(2,1)S(1)} collective-permute-done((bf16[16,1152]{1,0:T(8,128)(2,1)S(1)}, bf16[16,1152]{1,0:T(8,128)(2,1)S(1)}, u32[]{:S(2)}, u32[]{:S(2)}) %collective-permute-start) | collective-permute-done | bytes 36896 | tf_op jit(solution)/shard_map/ppermute | solution.py:164
  10.0 8.0 %all-gather = bf16[128,1152]{1,0:T(8,128)(2,1)S(1)} all-gather(bf16[32,1152]{1,0:T(8,128)(2,1)S(1)} %pad_maximum_fusion.7), channel_id=2, replica_groups=mesh['tile'=8,'tp'=4] {'tp'}, dimensions={0}, use_global_device_ids=true | all-gather | bytes 368640 | tf_op jit(solution)/shard_map/all_gather | solution.py:165
  18.7 0.9 copy-done.1
  20.7 0.9 pad_maximum_fusion.6
  22.3 3.3 %all-to-all-start = ((bf16[4,128,128]{2,1,0:T(8,128)(2,1)}), bf16[4,128,128]{2,1,0:T(8,128)(2,1)S(1)}, u32[]{:S(2)}, u32[]{:S(2)}) async-start(bf16[4,128,128]{2,1,0:T(8,128)(2,1)} %bitcast.58), calls=%async_computation | async-start | bytes 262144 | tf_op jit(solution)/shard_map/all_to_all | solution.py:185
  26.2 3.9 %all-to-all-done = bf16[4,128,128]{2,1,0:T(8,128)(2,1)S(1)} async-done(((bf16[4,128,128]{2,1,0:T(8,128)(2,1)}), bf16[4,128,128]{2,1,0:T(8,128)(2,1)S(1)}, u32[]{:S(2)}, u32[]{:S(2)}) %all-to-all-start) | async-done | bytes 131104 | tf_op jit(solution)/shard_map/all_to_all | solution.py:185
  30.2 1.0 add_convert_fusion
  31.7 1.0 convolution_convert_fusion.4.cot_ref
  32.7 6.3 %collective-permute-done.2 = bf16[128,1024]{1,0:T(8,128)(2,1)S(1)} collective-permute-done((bf16[128,1024]{1,0:T(8,128)(2,1)S(1)}, bf16[128,1024]{1,0:T(8,128)(2,1)S(1)}, u32[]{:S(2)}, u32[]{:S(2)}) %collective-permute-start.2) | collective-permute-done | bytes 262176 | tf_op jit(solution)/shard_map/ppermute | solution.py:30
  39.8 7.8 %conv_forward.1 = (bf16[96,512]{1,0:T(8,128)(2,1)}, bf16[64,512]{1,0:T(8,128)(2,1)}) custom-call(bf16[128,1024]{1,0:T(8,128)(2,1)} %fusion.14.rows_ref, f32[96,128]{1,0:T(8,128)} %fusion.52.table_ref, bf16[96,512]{1,0:T(8,128)(2,1)} %convolution_convert_fusion.4.cot_ref, bf16[7168,512]{1,0:T(8,128)(2,1)} %weight_ref.3), custom_call_target="tpu_custom_call" | custom-call | tf_op jit(solution)/shard_map/conv_forward/pallas_call | solution.py:99
  47.5 1.8 %convolution_convert_fusion.7 = bf16[64,512]{1,0:T(8,128)(2,1)} fusion(bf16[64,512]{1,0:T(8,128)(2,1)} %get-tuple-element.7, s32[512]{0:T(512)S(1)} %fusion.66), kind=kOutput, calls=%fused_computation.29 | convolution fusion | flops 33849344 | bytes 133120 | tf_op jit(solution)/shard_map/dot_general | solution.py:25
  49.3 3.3 %all-to-all-start.1 = ((bf16[4,16,512]{2,1,0:T(8,128)(2,1)}), bf16[4,16,512]{2,1,0:T(8,128)(2,1)S(1)}, u32[]{:S(2)}, u32[]{:S(2)}) async-start(bf16[4,16,512]{2,1,0:T(8,128)(2,1)} %bitcast.12), calls=%async_computation.1 | async-start | bytes 131072 | tf_op jit(solution)/shard_map/all_to_all | solution.py:270
  52.6 4.1 %all-to-all-done.1 = bf16[4,16,512]{2,1,0:T(8,128)(2,1)S(1)} async-done(((bf16[4,16,512]{2,1,0:T(8,128)(2,1)}), bf16[4,16,512]{2,1,0:T(8,128)(2,1)S(1)}, u32[]{:S(2)}, u32[]{:S(2)}) %all-to-all-start.1) | async-done | bytes 65568 | tf_op jit(solution)/shard_map/all_to_all | solution.py:270
  56.7 0.9 broadcast_in_dim.30
  57.6 5.8 %all-to-all-start.2 = ((bf16[8,32,1152]{2,1,0:T(8,128)(2,1)}), bf16[8,32,1152]{2,1,0:T(8,128)(2,1)S(1)}, u32[]{:S(2)}, u32[]{:S(2)}) async-start(bf16[8,32,1152]{2,1,0:T(8,128)(2,1)} %broadcast_in_dim.30), calls=%async_computation.2 | async-start | bytes 1179648 | tf_op jit(solution)/shard_map/all_to_all | solution.py:44
  64.0 8.2 %conv_backward.1 = bf16[64,1024]{1,0:T(8,128)(2,1)} custom-call(bf16[96,512]{1,0:T(8,128)(2,1)} %get-tuple-element.8.grad_ref, f32[96,128]{1,0:T(8,128)} %fusion.52.table_ref, s32[8,64]{1,0:T(8,128)} %broadcast_in_dim.28.order_ref, bf16[7168,512]{1,0:T(8,128)(2,1)} %weight_ref.3), custom_call_target="tpu_custom_call" | custom-call | tf_op jit(solution)/shard_map/conv_backward/pallas_call | solution.py:122
  72.3 0.9 slice.88
  73.2 1.3 collective-permute-done.4
  74.4 0.9 add_convert_fusion.2
  75.5 3.5 %all-to-all-done.2 = bf16[8,32,1152]{2,1,0:T(8,128)(2,1)S(1)} async-done(((bf16[8,32,1152]{2,1,0:T(8,128)(2,1)}), bf16[8,32,1152]{2,1,0:T(8,128)(2,1)S(1)}, u32[]{:S(2)}, u32[]{:S(2)}) %all-to-all-start.2) | async-done | bytes 589856 | tf_op jit(solution)/shard_map/all_to_all | solution.py:44
  79.1 0.9 broadcast_in_dim.34
  79.9 3.6 %all-to-all-start.4 = ((bf16[8,32,1024]{2,1,0:T(8,128)(2,1)}), bf16[8,32,1024]{2,1,0:T(8,128)(2,1)S(1)}, u32[]{:S(2)}, u32[]{:S(2)}) async-start(bf16[8,32,1024]{2,1,0:T(8,128)(2,1)} %broadcast_in_dim.34), calls=%async_computation.4 | async-start | bytes 1048576 | tf_op jit(solution)/shard_map/all_to_all | solution.py:44
  83.6 1.5 %fusion.83 = (bf16[32,1024]{1,0:T(8,128)(2,1)S(1)}, f32[32,1024]{1,0:T(8,128)}) fusion(bf16[32,1024]{1,0:T(8,128)(2,1)} %collective-permute-done.5, bf16[32,1024]{1,0:T(8,128)(2,1)} %copy-done.6), kind=kLoop, calls=%fused_computation.162 | loop fusion | flops 131072 | bytes 327680 | tf_op jit(solution)/shard_map/convert_element_type | solution.py:220
  87.0 3.1 %convolution_convert_fusion.3 = bf16[64,1024]{1,0:T(8,128)(2,1)S(1)} fusion(bf16[1024,1024]{1,0:T(8,128)(2,1)S(1)} %copy-done, bf16[1024,1024]{1,0:T(8,128)(2,1)} %param.9, f32[32,1024]{1,0:T(8,128)} %bitcast.81, f32[32,1024]{1,0:T(8,128)} %bitcast.80, bf16[32,1024]{1,0:T(8,128)(2,1)} %copy-done.9, bf16[32,1024]{1,0:T(8,128)(2,1)S(1)} %get-tuple-element.23), kind=kOutput, calls=%fused_computation.25 | convolution fusion | flops 269418496 | bytes 4718592 | tf_op jit(solution)/shard_map/dot_general | solution.py:25
  91.5 0.9 reshape.174
  93.1 0.9 add_convert_fusion.1
  94.7 3.5 %all-to-all-done.4 = bf16[8,32,1024]{2,1,0:T(8,128)(2,1)S(1)} async-done(((bf16[8,32,1024]{2,1,0:T(8,128)(2,1)}), bf16[8,32,1024]{2,1,0:T(8,128)(2,1)S(1)}, u32[]{:S(2)}, u32[]{:S(2)}) %all-to-all-start.4) | async-done | bytes 524320 | tf_op jit(solution)/shard_map/all_to_all | solution.py:44
  98.2 0.9 broadcast_in_dim.31
  99.1 4.2 %all-to-all-start.3 = ((bf16[8,32,1024]{2,1,0:T(8,128)(2,1)}), bf16[8,32,1024]{2,1,0:T(8,128)(2,1)}, u32[]{:S(2)}, u32[]{:S(2)}) async-start(bf16[8,32,1024]{2,1,0:T(8,128)(2,1)} %broadcast_in_dim.31), calls=%async_computation.3 | async-start | bytes 1048576 | tf_op jit(solution)/shard_map/all_to_all | solution.py:44
  103.3 1.7 %convolution_convert_fusion.5 = bf16[64,512]{1,0:T(8,128)(2,1)} fusion(bf16[8,8,4,128]{3,2,1,0:T(4,128)(2,1)} %bitcast.86, s32[64]{0:T(128)S(1)} %copy-done.10, s32[64]{0:T(128)S(1)} %fusion.73), kind=kOutput, calls=%fused_computation.27 | convolution fusion | flops 4231168 | bytes 131584 | tf_op jit(solution)/shard_map/dot_general | solution.py:25
  105.2 1.6 %fusion.47 = f32[16,1024]{1,0:T(8,128)} fusion(bf16[16,1024]{1,0:T(8,128)(2,1)S(1)} %copy-done.4, f32[32,1024]{1,0:T(8,128)} %get-tuple-element.24, s32[]{:T(128)S(6)} %select_n.173, bf16[16,1024]{1,0:T(8,128)(2,1)S(1)} %collective-permute-done.8, f32[16]{0:T(128)S(1)} %broadcast_multiply_fusion, f32[16]{0:T(128)S(1)} %add_rsqrt_fusion.1, ...), kind=kLoop, calls=%fused_computation.90 | loop fusion | flops 180224 | bytes 229512 | tf_op jit(solution)/shard_map/sub | solution.py:260
  107.3 10.2 %all-to-all-done.3 = bf16[8,32,1024]{2,1,0:T(8,128)(2,1)} async-done(((bf16[8,32,1024]{2,1,0:T(8,128)(2,1)}), bf16[8,32,1024]{2,1,0:T(8,128)(2,1)}, u32[]{:S(2)}, u32[]{:S(2)}) %all-to-all-start.3) | async-done | bytes 524320 | tf_op jit(solution)/shard_map/all_to_all | solution.py:44
  118.3 4.3 %all-to-all-start.5 = ((bf16[8,64,512]{2,1,0:T(8,128)(2,1)}), bf16[8,64,512]{2,1,0:T(8,128)(2,1)}, u32[]{:S(2)}, u32[]{:S(2)}) async-start(bf16[8,64,512]{2,1,0:T(8,128)(2,1)} %broadcast_in_dim.35), calls=%async_computation.5 | async-start | bytes 1048576 | tf_op jit(solution)/shard_map/all_to_all | solution.py:44
  122.8 1.2 pad_maximum_fusion
  124.2 0.9 broadcast_select_fusion.3
  125.8 2.6 %fusion.88 = f32[512,1024]{1,0:T(8,128)} fusion(bf16[512,1024]{1,0:T(8,128)(2,1)S(1)} %fusion.3, bf16[1024,1024]{1,0:T(8,128)(2,1)S(1)} %copy-done), kind=kOutput, calls=%fused_computation.165 | convolution fusion | flops 1073741824 | bytes 5242880 | tf_op jit(solution)/shard_map/dot_general | solution.py:25
  128.5 1.1 broadcast_select_fusion.1
  129.7 1.5 %convolution_convert_fusion = bf16[8,64,1024]{2,1,0:T(8,128)(2,1)} fusion(f32[8,64]{1,0:T(8,128)S(1)} %get-tuple-element.9, bf16[7,16,1024]{2,1,0:T(8,128)(2,1)S(1)} %get-tuple-element.16, bf16[7,16,1024]{2,1,0:T(8,128)(2,1)S(1)} %get-tuple-element.15, bf16[8,64,1024]{2,1,0:T(8,128)(2,1)S(1)} %bitcast.63), kind=kOutput, calls=%fused_computation.16 | convolution fusion | flops 109101056 | bytes 2557952 | tf_op jit(solution)/shard_map/dot_general | solution.py:315
  131.2 1.5 convolution_convert_fusion.1
  132.7 4.0 %all-to-all-done.5 = bf16[8,64,512]{2,1,0:T(8,128)(2,1)} async-done(((bf16[8,64,512]{2,1,0:T(8,128)(2,1)}), bf16[8,64,512]{2,1,0:T(8,128)(2,1)}, u32[]{:S(2)}, u32[]{:S(2)}) %all-to-all-start.5) | async-done | bytes 524320 | tf_op jit(solution)/shard_map/all_to_all | solution.py:44
  136.6 3.2 %convolution_multiply_fusion = f32[896,512]{1,0:T(8,128)} fusion(bf16[512,512]{1,0:T(8,128)(2,1)} %bitcast.31, s32[]{:T(128)S(6)} %select_n.191, bf16[512,1024]{1,0:T(8,128)(2,1)} %bitcast.93, bf16[512,1024]{1,0:T(8,128)(2,1)} %bitcast.92), kind=kOutput, calls=%fused_computation.15 | convolution fusion | flops 472055808 | bytes 4456452 | tf_op jit(solution)/shard_map/dot_general | solution.py:25
  139.9 1.3 pad_maximum_fusion.1
  141.2 4.9 %fusion.7 = f32[128,1024]{1,0:T(8,128)} fusion(f32[512,1024]{1,0:T(8,128)} %fusion.88, bf16[512,1024]{1,0:T(8,128)(2,1)S(1)} %bitcast.74, bf16[1024,1024]{1,0:T(8,128)(2,1)} %param.9, bf16[512,1024]{1,0:T(8,128)(2,1)} %copy-done.3, s32[]{:T(128)S(6)} %select_n.179), kind=kOutput, calls=%fused_computation.20 | convolution fusion | flops 1212809216 | bytes 5898244 | tf_op jit(solution)/shard_map/dot_general | solution.py:25
  146.1 3.1 %convolution_multiply_fusion.1 = f32[1024,128]{1,0:T(8,128)} fusion(f32[512,1024]{1,0:T(8,128)} %fusion.88, bf16[512,1024]{1,0:T(8,128)(2,1)S(1)} %bitcast.75, s32[]{:T(128)S(6)} %select_n.179), kind=kOutput, calls=%fused_computation.19 | convolution fusion | flops 136970240 | bytes 2752516 | tf_op jit(solution)/shard_map/dot_general | solution.py:25
  (87 shorter events, 14.7 us)
Async XLA Ops:
  0.6 17.5 %copy-start = (bf16[1024,1024]{1,0:T(8,128)(2,1)S(1)}, bf16[1024,1024]{1,0:T(8,128)(2,1)}, u32[]{:S(2)}) copy-start(bf16[1024,1024]{1,0:T(8,128)(2,1)} %param.8) | copy-start | bytes 6291460
  2.4 6.8 %collective-permute-start = (bf16[16,1152]{1,0:T(8,128)(2,1)S(1)}, bf16[16,1152]{1,0:T(8,128)(2,1)S(1)}, u32[]{:S(2)}, u32[]{:S(2)}) collective-permute-start(bf16[16,1152]{1,0:T(8,128)(2,1)S(1)} %pad_maximum_fusion.8), channel_id=1, source_target_pairs={{4,0},{5,1},{8,4},{9,5},{12,8},{13,9},{16,12},{17,13},{20,16},{21,... | collective-permute-start | bytes 110600 | tf_op jit(solution)/shard_map/ppermute | solution.py:164
  4.8 15.9 %collective-permute-start.3 = (bf16[64,512]{1,0:T(8,128)(2,1)S(1)}, bf16[64,512]{1,0:T(8,128)(2,1)}, u32[]{:S(2)}, u32[]{:S(2)}) collective-permute-start(bf16[64,512]{1,0:T(8,128)(2,1)S(1)} %convolution_convert_fusion.6), channel_id=1, source_target_pairs={{4,0},{8,4},{12,8},{16,12},{20,16},{24,20},{28,24},{3,7},{7,11},{1... | collective-permute-start | bytes 196616 | tf_op jit(solution)/shard_map/ppermute | solution.py:182
  18.0 1.6 %copy-start.1 = (bf16[1024,1024]{1,0:T(8,128)(2,1)S(1)}, bf16[1024,1024]{1,0:T(8,128)(2,1)}, u32[]{:S(2)}) copy-start(bf16[1024,1024]{1,0:T(8,128)(2,1)} %param.9) | copy-start | bytes 6291460
  19.6 0.8 copy-start.2
  20.3 9.8 %collective-permute-start.1 = (bf16[128,1024]{1,0:T(8,128)(2,1)S(1)}, bf16[128,1024]{1,0:T(8,128)(2,1)}, u32[]{:S(2)}, u32[]{:S(2)}) collective-permute-start(bf16[128,1024]{1,0:T(8,128)(2,1)S(1)} %convolution_convert_fusion.2), channel_id=1, source_target_pairs={{0,1},{1,0},{2,3},{3,2},{4,5},{5,4},{6,7},{7,6},{8,9},{9,8},{10,11... | collective-permute-start | bytes 786440 | tf_op jit(solution)/shard_map/ppermute | solution.py:30
  22.3 7.9 %all-to-all-start = ((bf16[4,128,128]{2,1,0:T(8,128)(2,1)}), bf16[4,128,128]{2,1,0:T(8,128)(2,1)S(1)}, u32[]{:S(2)}, u32[]{:S(2)}) async-start(bf16[4,128,128]{2,1,0:T(8,128)(2,1)} %bitcast.58), calls=%async_computation | async-start | bytes 262144 | tf_op jit(solution)/shard_map/all_to_all | solution.py:185
  31.2 7.7 %collective-permute-start.2 = (bf16[128,1024]{1,0:T(8,128)(2,1)S(1)}, bf16[128,1024]{1,0:T(8,128)(2,1)S(1)}, u32[]{:S(2)}, u32[]{:S(2)}) collective-permute-start(bf16[128,1024]{1,0:T(8,128)(2,1)S(1)} %add_convert_fusion), channel_id=1, source_target_pairs={{0,2},{1,3},{2,0},{3,1},{4,6},{5,7},{6,4},{7,5},{8,10},{9,11},{10,... | collective-permute-start | bytes 786440 | tf_op jit(solution)/shard_map/ppermute | solution.py:30
  49.3 7.4 %all-to-all-start.1 = ((bf16[4,16,512]{2,1,0:T(8,128)(2,1)}), bf16[4,16,512]{2,1,0:T(8,128)(2,1)S(1)}, u32[]{:S(2)}, u32[]{:S(2)}) async-start(bf16[4,16,512]{2,1,0:T(8,128)(2,1)} %bitcast.12), calls=%async_computation.1 | async-start | bytes 131072 | tf_op jit(solution)/shard_map/all_to_all | solution.py:270
  56.7 0.9 copy-start.8
  57.6 21.5 %all-to-all-start.2 = ((bf16[8,32,1152]{2,1,0:T(8,128)(2,1)}), bf16[8,32,1152]{2,1,0:T(8,128)(2,1)S(1)}, u32[]{:S(2)}, u32[]{:S(2)}) async-start(bf16[8,32,1152]{2,1,0:T(8,128)(2,1)} %broadcast_in_dim.30), calls=%async_computation.2 | async-start | bytes 1179648 | tf_op jit(solution)/shard_map/all_to_all | solution.py:44
  64.0 11.5 %slice-start = ((bf16[128,1024]{1,0:T(8,128)(2,1)}), bf16[64,1024]{1,0:T(8,128)(2,1)S(1)}, s32[]{:S(2)}) async-start(bf16[128,1024]{1,0:T(8,128)(2,1)} %fusion.14.rows_ref), calls=%async_computation.6 | async-start | bytes 262144 | tf_op jit(solution)/shard_map/slice | solution.py:233
  72.3 12.8 %slice-start.1 = ((f32[128,1024]{1,0:T(8,128)}), f32[64,1024]{1,0:T(8,128)S(1)}, s32[]{:S(2)}) async-start(f32[128,1024]{1,0:T(8,128)} %copy-done.2), calls=%async_computation.7 | async-start | bytes 524288 | tf_op jit(solution)/shard_map/slice | solution.py:240
  73.2 1.3 collective-permute-start.4
  75.3 8.3 %copy-start.6 = (bf16[32,1024]{1,0:T(8,128)(2,1)}, bf16[32,1024]{1,0:T(8,128)(2,1)S(1)}, u32[]{:S(2)}) copy-start(bf16[32,1024]{1,0:T(8,128)(2,1)S(1)} %add_convert_fusion.2) | copy-start | bytes 196612
  75.3 8.3 %collective-permute-start.5 = (bf16[32,1024]{1,0:T(8,128)(2,1)S(1)}, bf16[32,1024]{1,0:T(8,128)(2,1)}, u32[]{:S(2)}, u32[]{:S(2)}) collective-permute-start(bf16[32,1024]{1,0:T(8,128)(2,1)S(1)} %add_convert_fusion.2), channel_id=1, source_target_pairs={{0,2},{1,3},{2,0},{3,1},{4,6},{5,7},{6,4},{7,5},{8,10},{9,11},{10,... | collective-permute-start | bytes 196616 | tf_op jit(solution)/shard_map/ppermute | solution.py:30
  79.9 18.3 %all-to-all-start.4 = ((bf16[8,32,1024]{2,1,0:T(8,128)(2,1)}), bf16[8,32,1024]{2,1,0:T(8,128)(2,1)S(1)}, u32[]{:S(2)}, u32[]{:S(2)}) async-start(bf16[8,32,1024]{2,1,0:T(8,128)(2,1)} %broadcast_in_dim.34), calls=%async_computation.4 | async-start | bytes 1048576 | tf_op jit(solution)/shard_map/all_to_all | solution.py:44
  85.1 1.3 collective-permute-start.6
  86.4 0.6 copy-start.9
  87.0 3.9 %copy-start.5 = (bf16[96,512]{1,0:T(8,128)(2,1)S(1)}, bf16[96,512]{1,0:T(8,128)(2,1)}, u32[]{:S(2)}) copy-start(bf16[96,512]{1,0:T(8,128)(2,1)} %get-tuple-element.8.grad_ref) | copy-start | bytes 294916
  90.1 13.2 %copy-start.10 = (s32[64]{0:T(128)S(1)}, s32[64]{0:T(128)}, u32[]{:S(2)}) copy-start(s32[64]{0:T(128)} %param.12) | copy-start | bytes 772
  90.1 14.9 %copy-start.4 = (bf16[16,1024]{1,0:T(8,128)(2,1)S(1)}, bf16[16,1024]{1,0:T(8,128)(2,1)}, u32[]{:S(2)}) copy-start(bf16[16,1024]{1,0:T(8,128)(2,1)} %param.7) | copy-start | bytes 98308
  90.7 2.3 %collective-permute-start.7 = (bf16[32,1024]{1,0:T(8,128)(2,1)}, bf16[32,1024]{1,0:T(8,128)(2,1)}, u32[]{:S(2)}, u32[]{:S(2)}) collective-permute-start(bf16[32,1024]{1,0:T(8,128)(2,1)} %slice.91), channel_id=1, source_target_pairs={{0,1},{1,0},{2,3},{3,2},{4,5},{5,4},{6,7},{7,6},{8,9},{9,8},{10,11... | collective-permute-start | bytes 196616 | tf_op jit(solution)/shard_map/ppermute | solution.py:30
  93.9 23.6 %copy-start.7 = (bf16[64,512]{1,0:T(8,128)(2,1)S(1)}, bf16[64,512]{1,0:T(8,128)(2,1)}, u32[]{:S(2)}) copy-start(bf16[64,512]{1,0:T(8,128)(2,1)} %slice.79) | copy-start | bytes 196612
  94.0 11.1 %collective-permute-start.8 = (bf16[16,1024]{1,0:T(8,128)(2,1)S(1)}, bf16[16,1024]{1,0:T(8,128)(2,1)S(1)}, u32[]{:S(2)}, u32[]{:S(2)}) collective-permute-start(bf16[16,1024]{1,0:T(8,128)(2,1)S(1)} %constant_dynamic-slice_fusion.2), channel_id=1, source_target_pairs={{0,2},{1,3},{2,0},{3,1},{4,6},{5,7},{6,4},{7,5},{8,10},{9,11},{10,... | collective-permute-start | bytes 98312 | tf_op jit(solution)/shard_map/ppermute | solution.py:30
  99.1 18.4 %all-to-all-start.3 = ((bf16[8,32,1024]{2,1,0:T(8,128)(2,1)}), bf16[8,32,1024]{2,1,0:T(8,128)(2,1)}, u32[]{:S(2)}, u32[]{:S(2)}) async-start(bf16[8,32,1024]{2,1,0:T(8,128)(2,1)} %broadcast_in_dim.31), calls=%async_computation.3 | async-start | bytes 1048576 | tf_op jit(solution)/shard_map/all_to_all | solution.py:44
  105.1 17.6 %collective-permute-start.9 = (bf16[8,32,1152]{2,1,0:T(8,128)(2,1)S(1)}, bf16[8,32,1152]{2,1,0:T(8,128)(2,1)}, u32[]{:S(2)}, u32[]{:S(2)}) collective-permute-start(bf16[8,32,1152]{2,1,0:T(8,128)(2,1)S(1)} %all-to-all-done.2), channel_id=1, source_target_pairs={{0,1},{1,0},{2,3},{3,2},{4,5},{5,4},{6,7},{7,6},{8,9},{9,8},{10,11... | collective-permute-start | bytes 1769480 | tf_op jit(solution)/shard_map/ppermute | solution.py:30
  106.8 21.7 %collective-permute-start.11 = (bf16[8,32,1024]{2,1,0:T(8,128)(2,1)S(1)}, bf16[8,32,1024]{2,1,0:T(8,128)(2,1)}, u32[]{:S(2)}, u32[]{:S(2)}) collective-permute-start(bf16[8,32,1024]{2,1,0:T(8,128)(2,1)S(1)} %all-to-all-done.4), channel_id=1, source_target_pairs={{0,1},{1,0},{2,3},{3,2},{4,5},{5,4},{6,7},{7,6},{8,9},{9,8},{10,11... | collective-permute-start | bytes 1572872 | tf_op jit(solution)/shard_map/ppermute | solution.py:30
  118.3 18.3 %all-to-all-start.5 = ((bf16[8,64,512]{2,1,0:T(8,128)(2,1)}), bf16[8,64,512]{2,1,0:T(8,128)(2,1)}, u32[]{:S(2)}, u32[]{:S(2)}) async-start(bf16[8,64,512]{2,1,0:T(8,128)(2,1)} %broadcast_in_dim.35), calls=%async_computation.5 | async-start | bytes 1048576 | tf_op jit(solution)/shard_map/all_to_all | solution.py:44
  122.7 17.2 %collective-permute-start.10 = (bf16[8,32,1024]{2,1,0:T(8,128)(2,1)}, bf16[8,32,1024]{2,1,0:T(8,128)(2,1)}, u32[]{:S(2)}, u32[]{:S(2)}) collective-permute-start(bf16[8,32,1024]{2,1,0:T(8,128)(2,1)} %all-to-all-done.3), channel_id=1, source_target_pairs={{0,1},{1,0},{2,3},{3,2},{4,5},{5,4},{6,7},{7,6},{8,9},{9,8},{10,11... | collective-permute-start | bytes 1572872 | tf_op jit(solution)/shard_map/ppermute | solution.py:30
  125.8 2.6 %copy-start.3 = (bf16[512,1024]{1,0:T(8,128)(2,1)}, bf16[512,1024]{1,0:T(8,128)(2,1)S(1)}, u32[]{:S(2)}) copy-start(bf16[512,1024]{1,0:T(8,128)(2,1)S(1)} %fusion.3) | copy-start | bytes 3145732
